TPU v7x, 128 devices: a whole 4x4x4 slice. The times are simulated.
128 devices in a mesh: gx: 8 (over x, core), gy: 16 (over z, y).
Axes of the slice: x: 4, y: 4, z: 4, core: 2. Of those that a mesh axis runs over, the one named last changes fastest.
Arguments:
- velocity: float32 [3, 2, 2048, 2048], P(None, None, 'gx', 'gy'), may hold values from -20 to 20
- viscosity: float32 [2, 2048, 2048], P(None, 'gx', 'gy'), may hold values from 1 to 16
Outputs:
- velocity_new: float32 [3, 2, 2048, 2048], P(None, None, 'gx', 'gy')
All inputs are finite; a program needn't handle non-finite values.
Results may differ from a plain program's by a relative error of at most 0.00035.
Values sent between devices are 32-bit elements; how exact they have to be, the bound alone decides.
A program may use at most 64 MiB of HBM per device.

v0:
```python
import jax
import jax.numpy as jnp
from jax import lax
from jax.sharding import PartitionSpec as P

diffusion = 10000.0


def in_one_piece(arrays, axis, dim, along):
    ends, at = ([], 0)
    for a in arrays[:-1]:
        at += a.shape[along]
        ends.append(at)
    both = jnp.concatenate(arrays, axis=along)
    return tuple(jnp.split(lax.all_gather(both, axis, axis=dim, tiled=True), ends, axis=along))


def thomas(coeffs, rights):
    coupling = diffusion * coeffs

    def forward(carry, item):
        prev_c, prev_d = carry
        couple_row, right_row = item
        pivot = 1.0 + 2.0 * couple_row + couple_row * prev_c
        new_c = -couple_row / pivot
        new_d = (right_row + couple_row * prev_d) / pivot
        return ((new_c, new_d), (new_c, new_d))

    start = (jnp.zeros_like(coupling[0]), jnp.zeros_like(rights[0]))
    _, (c_all, d_all) = lax.scan(forward, start, (coupling, rights), unroll=8)

    def backward(later, item):
        upper_row, value_row = item
        result = value_row - upper_row * later
        return (result, result)

    _, solved = lax.scan(
        backward, jnp.zeros_like(rights[0]), (c_all, d_all), reverse=True, unroll=8
    )
    return solved


def edge_terms(coeffs):
    length = coeffs.shape[0]
    coupling = diffusion * coeffs
    places = lax.broadcasted_iota(jnp.int32, coeffs.shape, 0)
    nothing = jnp.zeros_like(coupling)
    first_side = jnp.where(places == 0, coupling, nothing)
    last_side = jnp.where(places == length - 1, coupling, nothing)
    return jnp.concatenate([first_side, last_side], axis=1)


def reduced_rows(solved):
    first_row = solved[0]
    last_row = solved[-1]
    values = jnp.stack([first_row[:3], last_row[:3]])
    nothing = jnp.zeros_like(first_row[3])
    lower_map = jnp.stack([jnp.stack([nothing, first_row[3]]), jnp.stack([nothing, last_row[3]])])
    upper_map = jnp.stack([jnp.stack([first_row[4], nothing]), jnp.stack([last_row[4], nothing])])
    return (values, lower_map, upper_map)


def mat_prod(left_mat, right_mat):
    return (
        left_mat[..., :, 0:1, :, :] * right_mat[..., 0:1, :, :, :]
        + left_mat[..., :, 1:2, :, :] * right_mat[..., 1:2, :, :, :]
    )


def invert(matrix):
    upper_left = matrix[..., 0:1, 0:1, :, :]
    upper_right = matrix[..., 0:1, 1:2, :, :]
    lower_left = matrix[..., 1:2, 0:1, :, :]
    lower_right = matrix[..., 1:2, 1:2, :, :]
    determinant = upper_left * lower_right - upper_right * lower_left
    top_half = jnp.concatenate([lower_right, -upper_right], axis=-3)
    bottom_half = jnp.concatenate([-lower_left, upper_left], axis=-3)
    return jnp.concatenate([top_half, bottom_half], axis=-4) / determinant


def reduce_step(values, lower_map, upper_map, below, above):
    identity = jnp.eye(2, dtype=values.dtype)[:, :, None, None]
    system = identity - mat_prod(lower_map, below[2]) - mat_prod(upper_map, above[1])
    inverse = invert(system)
    new_values = mat_prod(
        inverse, values + mat_prod(lower_map, below[0]) + mat_prod(upper_map, above[0])
    )
    new_lower = mat_prod(inverse, mat_prod(lower_map, below[1]))
    new_upper = mat_prod(inverse, mat_prod(upper_map, above[2]))
    return (new_values, new_lower, new_upper)


def shift_down(array, span):
    return jnp.concatenate([jnp.zeros_like(array[:span]), array[:-span]], axis=0)


def shift_up(array, span):
    return jnp.concatenate([array[span:], jnp.zeros_like(array[:span])], axis=0)


def solve_collected(values, lower_map, upper_map, position):
    devices = values.shape[0]
    span = 1
    while span < devices:
        below = (shift_down(values, span), shift_down(lower_map, span), shift_down(upper_map, span))
        above = (shift_up(values, span), shift_up(lower_map, span), shift_up(upper_map, span))
        values, lower_map, upper_map = reduce_step(values, lower_map, upper_map, below, above)
        span = span * 2
    padded = jnp.concatenate(
        [jnp.zeros_like(values[:1]), values, jnp.zeros_like(values[:1])], axis=0
    )
    left_row = lax.dynamic_slice_in_dim(padded, position, 1, 0)[0]
    right_row = lax.dynamic_slice_in_dim(padded, position + 2, 1, 0)[0]
    return (left_row[1], right_row[0])


def combine(solved, left_end, right_end):
    return solved[:, :3] + solved[:, 3:4] * left_end[None] + solved[:, 4:5] * right_end[None]


def on_device(velocity, viscosity):
    kappa_x = jnp.moveaxis(viscosity, 1, 0)[:, None]
    lines = jnp.moveaxis(velocity, 2, 0)
    solved = thomas(kappa_x, jnp.concatenate([lines, edge_terms(kappa_x)], axis=1))
    values, lower_map, upper_map = reduced_rows(solved)
    all_values, all_lower, all_upper = in_one_piece(
        (values[None], lower_map[None], upper_map[None]), "gx", 0, 2
    )
    left_end, right_end = solve_collected(all_values, all_lower, all_upper, lax.axis_index("gx"))
    xsolved = combine(solved, left_end, right_end)
    ylines = xsolved.transpose(3, 1, 2, 0)
    kappa_y = viscosity.transpose(2, 0, 1)[:, None]
    solved_y = thomas(kappa_y, jnp.concatenate([ylines, edge_terms(kappa_y)], axis=1))
    values_y, lower_y, upper_y = reduced_rows(solved_y)
    all_values, all_lower, all_upper = in_one_piece(
        (values_y[None], lower_y[None], upper_y[None]), "gy", 0, 2
    )
    left_y, right_y = solve_collected(all_values, all_lower, all_upper, lax.axis_index("gy"))
    return combine(solved_y, left_y, right_y).transpose(1, 2, 3, 0)


def solution(mesh):
    return jax.shard_map(
        on_device,
        mesh=mesh,
        in_specs=(P(None, None, "gx", "gy"), P(None, "gx", "gy")),
        out_specs=P(None, None, "gx", "gy"),
        check_vma=False,
    )
```

profile of v0, /device:TPU:0, one launch (start us, length us, event | category | flops | bytes accessed | tf_op | source)
XLA Modules:
  0.0 139.6 jit_solution(15989872752286631089)
XLA Ops:
  0.0 1.2 broadcast_select_fusion.3
  3.5 35.4 %while.68 = (s32[]{:T(128)}, f32[1,2,128]{2,1,0:T(2,128)S(1)}, f32[5,2,128]{2,1,0:T(2,128)S(1)}, f32[32,8,1,2,128]{4,3,1,2,0:T(2,128)}, f32[32,8,5,2,128]{4,3,2,...) while((s32[]{:T(128)}, f32[1,2,128]{2,1,0:T(2,128)S(1)}, ...), condition=%wide.region_1.2_spmd.clone, body=%wide.region_0.1_spmd.clone.sunk | while | flops 69640 | bytes 361406 | solution.py:30
  39.0 33.2 %while.69 = (s32[]{:T(128)}, f32[5,2,128]{2,1,0:T(2,128)S(1)}, f32[32,8,5,2,128]{4,1,0,3,2:T(8,128)S(1)}, f32[32,8,5,2,128]{4,3,2,1,0:T(2,128)S(1)}, f32[32,8,1,...) while((s32[]{:T(128)}, f32[5,2,128]{2,1,0:T(2,128)S(1)}, ...), condition=%wide.region_3.4_spmd.clone, body=%wide.region_2.3_spmd.clone.sunk | while | flops 33290 | bytes 285020 | solution.py:37
  39.0 0.8 fusion.314
  40.1 0.8 fusion.314
  41.1 0.8 fusion.314
  42.1 0.8 fusion.314
  43.2 0.8 fusion.314
  44.2 0.8 fusion.314
  45.2 0.8 fusion.314
  47.3 0.8 fusion.314
  48.3 0.8 fusion.314
  49.4 0.8 fusion.314
  50.4 0.8 fusion.314
  51.5 0.8 fusion.314
  52.5 0.8 fusion.314
  53.5 0.8 fusion.314
  54.6 0.8 fusion.314
  55.6 0.8 fusion.314
  56.6 0.8 fusion.314
  57.7 0.8 fusion.314
  58.7 0.8 fusion.314
  59.7 0.8 fusion.314
  60.8 0.8 fusion.314
  61.8 0.8 fusion.314
  62.9 0.8 fusion.314
  63.9 0.8 fusion.314
  72.4 13.2 %all_gather.6 = f32[8,2,7,2,128]{4,3,2,1,0:T(2,128)S(1)} all-gather(f32[1,2,7,2,128]{4,3,2,1,0:T(2,128)S(1)} %copy.443), channel_id=1, replica_groups=mesh['gx'=8,'gy'=16] {'gx'}, dimensions={0}, use_global_device_ids=true | all-gather | bytes 129024 | tf_op jit(solution)/shard_map/all_gather | solution.py:15
  88.6 10.9 %while.70 = (s32[]{:T(128)}, f32[1,2,256]{2,1,0:T(2,128)S(1)}, f32[5,2,256]{2,1,0:T(2,128)S(1)}, f32[16,8,1,2,256]{4,3,1,2,0:T(2,128)S(1)}, f32[16,8,5,2,256]{4,...) while((s32[]{:T(128)}, f32[1,2,256]{2,1,0:T(2,128)S(1)}, ...), condition=%wide.region_5.6_spmd.clone, body=%wide.region_4.5_spmd.clone.sunk | while | flops 139272 | bytes 885146 | solution.py:30
  99.5 4.9 %while.71 = (s32[]{:T(128)}, f32[5,2,256]{2,1,0:T(2,128)S(1)}, f32[16,8,5,2,256]{4,1,0,3,2:T(8,128)S(1)}, f32[16,8,5,2,256]{4,3,2,1,0:T(2,128)S(1)}, f32[16,8,1,...) while((s32[]{:T(128)}, f32[5,2,256]{2,1,0:T(2,128)S(1)}, ...), condition=%wide.region_7.8_spmd.clone, body=%wide.region_6.7_spmd.clone.sunk | while | flops 66570 | bytes 569692 | solution.py:37
  104.6 26.0 %all_gather.7 = f32[16,2,7,2,256]{4,3,2,1,0:T(2,128)S(1)} all-gather(f32[1,2,7,2,256]{4,3,2,1,0:T(2,128)S(1)} %copy.481), channel_id=1, replica_groups=mesh['gx'=8,'gy'=16] {'gy'}, dimensions={0}, use_global_device_ids=true | all-gather | bytes 487424 | tf_op jit(solution)/shard_map/all_gather | solution.py:15
  138.5 1.1 copy.527
  (1728 shorter events, 69.7 us)
Async XLA Ops:
  0.0 1.6 %copy-start.1 = (f32[3,2,256,128]{3,2,1,0:T(8,128)S(1)}, f32[3,2,256,128]{3,2,1,0:T(8,128)}, u32[]{:S(2)}) copy-start(f32[3,2,256,128]{3,2,1,0:T(8,128)} %param.10) | copy-start | bytes 2359300
  2.2 1.0 copy-start
where the time goes:
time: 140 us
  local copies, waits for them, and re-layouts  58.7 us (42%)
  blocking collectives  39.3 us (28%)
  other arithmetic  32.8 us (23%)
  loops' own time  7.09 us (5%)
  between operations  1.81 us (1%)
    all_gather x2, blocking collectives, in_one_piece(): lax.all_gather(both, axis, axis=dim, tiled=True)  39.3 us
    mul x48, local copies, waits for them, and re-layouts, backward(): result = value_row - upper_row * later  26.4 us
    dynamic_update_slice x144, local copies, waits for them, and re-layouts, thomas(): _, (c_all, d_all) = lax.scan(forward, start, (coupling, rights), unroll=8)  21.1 us
    while x864, other arithmetic  20.2 us
    another operation x2, loops' own time, thomas(): _, (c_all, d_all) = lax.scan(forward, start, (coupling, rights), unroll=8)  3.78 us
    another operation x2, loops' own time, thomas(): lax.scan(backward, jnp.zeros_like(rights[0]), (c_all, d_all), reverse=Tru...  3.31 us

commit v1 on v0

v1 whole, which is shorter than its diff:
```python
import functools

import jax
import jax.numpy as jnp
from jax import lax
from jax.experimental import pallas as pl
from jax.experimental.pallas import tpu as pltpu
from jax.sharding import PartitionSpec as P

diffusion = 10000.0
MESH = pl.DeviceIdType.MESH
CH = 8
LANES = 128


def row8(ref_or_value):
    return jnp.broadcast_to(ref_or_value, (CH, LANES))


def fundamental(load_eps, phi, psi, ends, cols, steps):
    one = jnp.ones((CH, LANES), jnp.float32)
    zero = jnp.zeros((CH, LANES), jnp.float32)
    state = [(one, zero, zero, one) for _ in range(cols)]
    for t in range(steps):
        for col in range(cols):
            a, da, b, db = state[col]
            phi[col, t] = a
            psi[col, t] = b
            e = load_eps(col, t)
            da = da + e * a
            db = db + e * b
            state[col] = (a + da, da, b + db, db)
    for col in range(cols):
        a, da, b, db = state[col]
        ends[0, col] = a
        ends[1, col] = b
        ends[2, col] = da
        ends[3, col] = db


def chunk_states(ends, states, coef, cols):
    one = jnp.ones((cols, LANES), jnp.float32)
    zero = jnp.zeros((cols, LANES), jnp.float32)
    f, df, m, v = one, zero, zero, one
    n, z = zero, one
    for q in range(CH):
        a, b, da, db = [ends[k, :, q, :] for k in range(4)]
        states[0, :, q, :] = m
        states[1, :, q, :] = v
        f, df = a * f + b * df, da * f + db * df
        m, v = a * m + b * v, da * m + db * v
        r = CH - 1 - q
        a, b, da, db = [ends[k, :, r, :] for k in range(4)]
        n, z = db * n + b * z, a * z + da * n
        states[2, :, r, :] = n
        states[3, :, r, :] = z
    coef[0 * cols : 1 * cols, :] = f
    coef[1 * cols : 2 * cols, :] = m
    coef[2 * cols : 3 * cols, :] = df
    coef[3 * cols : 4 * cols, :] = v
    return m, 1.0 / m


def weights(load_eps, phi, psi, aw, bw, states, whole, inverse, cols, steps):
    for col in range(cols):
        w = row8(whole[col : col + 1, :])
        k = row8(inverse[col : col + 1, :])
        ms, vs, ns, zs = [states[j, col] * k for j in range(4)]
        for t in range(steps):
            a = phi[col, t]
            b = psi[col, t]
            we = load_eps(col, t) * w
            alpha = ns * a - zs * b
            beta = ms * a + vs * b
            phi[col, t] = alpha
            psi[col, t] = beta
            aw[col, t] = alpha * we
            bw[col, t] = beta * we


def totals(load_f, aw, bw, cols, steps, col):
    zero = jnp.zeros((CH, LANES), jnp.float32)
    left = [zero] * 3
    right = [zero] * 3
    for t in range(steps):
        a = aw[col, t]
        b = bw[col, t]
        for c in range(3):
            f = load_f(c, col, t)
            left[c] = left[c] + a * f
            right[c] = right[c] + b * f
    return left, right


def scan_up(x, places):
    for d in (1, 2, 4):
        x = x + jnp.where(places >= d, pltpu.roll(x, d, 0), 0.0)
    return x


def scan_down(x, places):
    for d in (1, 2, 4):
        x = x + jnp.where(places < CH - d, pltpu.roll(x, CH - d, 0), 0.0)
    return x


def interior(load_f, alpha, beta, aw, bw, tots, part, cols, steps):
    places = lax.broadcasted_iota(jnp.int32, (CH, LANES), 0)
    for col in range(cols):
        pre, suf = [], []
        for c in range(3):
            left = tots[0, c, col]
            right = tots[1, c, col]
            pre.append(scan_up(right, places) - right)
            suf.append(scan_down(left, places))
        for t in range(steps):
            a, b = aw[col, t], bw[col, t]
            al, be = alpha[col, t], beta[col, t]
            for c in range(3):
                f = load_f(c, col, t)
                pre[c] = pre[c] + b * f
                suf[c] = suf[c] - a * f
                part[c, col, t] = al * pre[c] + be * suf[c]


def green(coef, nodes, wts, me, devices, rows):
    m = jnp.ones((rows, LANES), jnp.float32)
    v = m
    n = jnp.zeros((rows, LANES), jnp.float32)
    z = jnp.ones((rows, LANES), jnp.float32)
    ms, ns = [m], [n]
    nodes[0, 0] = m
    nodes[1, devices] = n
    for p in range(devices):
        a, b, da, db = [coef[p, k * rows : (k + 1) * rows, :] for k in range(4)]
        m, v = a * m + b * v, da * m + db * v
        ms.append(m)
        nodes[0, p + 1] = m
        r = devices - 1 - p
        a, b, da, db = [coef[r, k * rows : (k + 1) * rows, :] for k in range(4)]
        n, z = db * n + b * z, a * z + da * n
        ns.append(n)
        nodes[1, r] = n
    ns = ns[::-1]
    inverse = 1.0 / m
    for side in range(2):
        at = me + side
        mm = nodes[0, at] * inverse
        nn = nodes[1, at] * inverse
        g = [jnp.where(p <= at, ms[p] * nn, ns[p] * mm) for p in range(devices + 1)]
        for p in range(devices):
            pair = [g[p], g[p + 1]] * (CH // (2 * rows))
            wts[side, p] = jnp.concatenate(pair, axis=0)


def kernel(
    nx, ny, sx, sy,
    visc_hbm, vel_hbm, out_hbm,
    visc, vel, eps, eps_t, out,
    xphi, xpsi, xaw, xbw, xends, xstates, xtots, xpart, xnodes, xwts, xcoef, xsrc,
    yphi, ypsi, yaw, ybw, yends, ystates, ytots, ypart, ynodes, ywts, ycoef, ysrc,
    ut, in_sem, out_sem,
    xc_send, xc_recv, xs_send, xs_recv, yc_send, yc_recv, ys_send, ys_recv,
):
    gx = lax.axis_index("gx")
    gy = lax.axis_index("gy")
    loads = [pltpu.make_async_copy(visc_hbm.at[z], visc.at[z], in_sem.at[z]) for z in range(2)]
    for c in range(3):
        for z in range(2):
            loads.append(
                pltpu.make_async_copy(
                    vel_hbm.at[c, z], vel.at[c, z], in_sem.at[2 + 2 * c + z]
                )
            )
    for copy in loads:
        copy.start()
    barrier = pltpu.get_barrier_semaphore()
    for d in range(1, nx):
        pl.semaphore_signal(
            barrier, inc=1, device_id={"gx": lax.rem(gx + d, nx)}, device_id_type=MESH
        )
    for d in range(1, ny):
        pl.semaphore_signal(
            barrier, inc=1, device_id={"gy": lax.rem(gy + d, ny)}, device_id_type=MESH
        )

    def share(axis, me, devices, buf, send, recv):
        copies = []
        for d in range(1, devices):
            peer = lax.rem(me + d, devices)
            copy = pltpu.make_async_remote_copy(
                src_ref=buf.at[me],
                dst_ref=buf.at[me],
                send_sem=send.at[d - 1],
                recv_sem=recv.at[me],
                device_id={axis: peer},
                device_id_type=MESH,
            )
            copy.start()
            copies.append(copy)
        return copies

    def arrive(axis, me, devices, buf, send, recv):
        for d in range(1, devices):
            peer = lax.rem(me + d, devices)
            pltpu.make_async_remote_copy(
                src_ref=buf.at[peer],
                dst_ref=buf.at[peer],
                send_sem=send.at[d - 1],
                recv_sem=recv.at[peer],
                device_id={axis: peer},
                device_id_type=MESH,
            ).wait_recv()

    for copy in loads[:2]:
        copy.wait()
    for z in range(2):
        eps[z] = 1.0 / (diffusion * visc[z])

    def eps_x(col, t):
        return eps[col, pl.ds(t, CH, stride=sx), :]

    def vel_x(c, col, t):
        return vel[c, col, pl.ds(t, CH, stride=sx), :]

    def eps_y(col, t):
        return eps_t[col, pl.ds(t, CH, stride=sy), :]

    def vel_y(c, col, t):
        return ut[c, col, pl.ds(t, CH, stride=sy), :]

    fundamental(eps_x, xphi, xpsi, xends, 2, sx)
    xwhole, xinv = chunk_states(xends, xstates, xcoef.at[gx], 2)
    pl.semaphore_wait(barrier, nx + ny - 2)
    sent = share("gx", gx, nx, xcoef, xc_send, xc_recv)
    weights(eps_x, xphi, xpsi, xaw, xbw, xstates, xwhole, xinv, 2, sx)
    for copy in loads[2:]:
        copy.wait()
    for col in range(2):
        left, right = totals(vel_x, xaw, xbw, 2, sx, col)
        k = xinv[col : col + 1, :]
        for c in range(3):
            xtots[0, c, col] = left[c]
            xtots[1, c, col] = right[c]
            for lr, value in enumerate((left[c], right[c])):
                at = (c % 2) * 4 + lr * 2 + col
                row = k * jnp.sum(value, axis=0, keepdims=True)
                xsrc[gx, c // 2, at : at + 1, :] = row
    xsrc[gx, 1, 4:8, :] = jnp.zeros((4, LANES), jnp.float32)
    sent += share("gx", gx, nx, xsrc, xs_send, xs_recv)

    for z in range(2):
        for tile in range(2):
            eps_t[2 * z + tile] = eps[z, tile * LANES : (tile + 1) * LANES, :].T
    fundamental(eps_y, yphi, ypsi, yends, 4, sy)
    ywhole, yinv = chunk_states(yends, ystates, ycoef.at[gy], 4)
    sent += share("gy", gy, ny, ycoef, yc_send, yc_recv)
    interior(vel_x, xphi, xpsi, xaw, xbw, xtots, xpart, 2, sx)
    weights(eps_y, yphi, ypsi, yaw, ybw, ystates, ywhole, yinv, 4, sy)
    arrive("gx", gx, nx, xcoef, xc_send, xc_recv)
    green(xcoef, xnodes, xwts, gx, nx, 2)

    arrive("gx", gx, nx, xsrc, xs_send, xs_recv)
    ends = []
    for side in range(2):
        tiles = []
        for k in range(2):
            acc = xwts[side, 0] * xsrc[0, k]
            for p in range(1, nx):
                acc = acc + xwts[side, p] * xsrc[p, k]
            tiles.append(acc + pltpu.roll(acc, CH - 2, 0))
        ends.append(tiles)
    for col in range(2):
        for c in range(3):
            at = (c % 2) * 4 + col
            s = row8(ends[0][c // 2][at : at + 1, :])
            r = row8(ends[1][c // 2][at : at + 1, :])
            for t in range(sx):
                vel[c, col, pl.ds(t, CH, stride=sx), :] = (
                    xpart[c, col, t] + xphi[col, t] * s + xpsi[col, t] * r
                )

    for col in range(4):
        z, tile = col // 2, col % 2
        for c in range(3):
            ut[c, col] = vel[c, z, tile * LANES : (tile + 1) * LANES, :].T
        left, right = totals(vel_y, yaw, ybw, 4, sy, col)
        k = yinv[col : col + 1, :]
        for c in range(3):
            ytots[0, c, col] = left[c]
            ytots[1, c, col] = right[c]
            for lr, value in enumerate((left[c], right[c])):
                at = lr * 4 + col
                ysrc[gy, c, at : at + 1, :] = k * jnp.sum(value, axis=0, keepdims=True)
    sent += share("gy", gy, ny, ysrc, ys_send, ys_recv)
    arrive("gy", gy, ny, ycoef, yc_send, yc_recv)
    green(ycoef, ynodes, ywts, gy, ny, 4)
    interior(vel_y, yphi, ypsi, yaw, ybw, ytots, ypart, 4, sy)

    arrive("gy", gy, ny, ysrc, ys_send, ys_recv)
    ends = []
    for side in range(2):
        tiles = []
        for c in range(3):
            acc = ywts[side, 0] * ysrc[0, c]
            for p in range(1, ny):
                acc = acc + ywts[side, p] * ysrc[p, c]
            tiles.append(acc + pltpu.roll(acc, 4, 0))
        ends.append(tiles)
    stores = []
    for c in range(3):
        for z in range(2):
            for tile in range(2):
                col = 2 * z + tile
                s = row8(ends[0][c][col : col + 1, :])
                r = row8(ends[1][c][col : col + 1, :])
                for t in range(sy):
                    ut[c, col, pl.ds(t, CH, stride=sy), :] = (
                        ypart[c, col, t] + yphi[col, t] * s + ypsi[col, t] * r
                    )
                out[c, z, tile * LANES : (tile + 1) * LANES, :] = ut[c, col].T
            store = pltpu.make_async_copy(out.at[c, z], out_hbm.at[c, z], out_sem.at[2 * c + z])
            store.start()
            stores.append(store)
    for copy in sent:
        copy.wait_send()
    for store in stores:
        store.wait()


def on_device(nx, ny, velocity, viscosity):
    lx, ly = velocity.shape[2], velocity.shape[3]
    sx, sy = lx // CH, ly // CH
    f32 = jnp.float32
    vm = lambda *shape: pltpu.VMEM(shape, f32)
    dma = lambda n: pltpu.SemaphoreType.DMA((n,))

    def phase(cols, steps, devices, rows, coefs, srcs):
        return [
            vm(cols, steps, CH, LANES),
            vm(cols, steps, CH, LANES),
            vm(cols, steps, CH, LANES),
            vm(cols, steps, CH, LANES),
            vm(4, cols, CH, LANES),
            vm(4, cols, CH, LANES),
            vm(2, 3, cols, CH, LANES),
            vm(3, cols, steps, CH, LANES),
            vm(2, devices + 1, rows, LANES),
            vm(2, devices, CH, LANES),
            vm(devices, coefs, LANES),
            vm(devices, srcs, CH, LANES),
        ]

    return pl.pallas_call(
        functools.partial(kernel, nx, ny, sx, sy),
        out_shape=jax.ShapeDtypeStruct(velocity.shape, f32),
        in_specs=[pl.BlockSpec(memory_space=pl.ANY)] * 2,
        out_specs=pl.BlockSpec(memory_space=pl.ANY),
        scratch_shapes=[
            vm(2, lx, ly),
            vm(3, 2, lx, ly),
            vm(2, lx, ly),
            vm(4, ly, LANES),
            vm(3, 2, lx, ly),
            *phase(2, sx, nx, 2, 8, 2),
            *phase(4, sy, ny, 4, 16, 3),
            vm(3, 4, ly, LANES),
            dma(8),
            dma(6),
            dma(nx), dma(nx), dma(nx), dma(nx),
            dma(ny), dma(ny), dma(ny), dma(ny),
        ],
        compiler_params=pltpu.CompilerParams(collective_id=0, has_side_effects=True),
    )(viscosity, velocity)


def solution(mesh):
    return jax.shard_map(
        functools.partial(on_device, mesh.shape["gx"], mesh.shape["gy"]),
        mesh=mesh,
        in_specs=(P(None, None, "gx", "gy"), P(None, "gx", "gy")),
        out_specs=P(None, None, "gx", "gy"),
        check_vma=False,
    )
```

time: 140 us -> 22.6 us (0.16)
  the two profiles are of different devices: /device:TPU:0 before, /device:TPU:1 now
where the time goes in v1:
time: 22.6 us; the launch traced here: 22.4 us
  Pallas kernels  20.3 us (90%)
  local copies, waits for them, and re-layouts  2.06 us (9%)
    pallas_call x1, Pallas kernels, on_device(): pl.pallas_call(functools.partial(kernel, nx, ny, sx, sy), out_shape=jax.S...  20.3 us
    unnamed x1, local copies, waits for them, and re-layouts  2.06 us

profile of v1, /device:TPU:1, one launch (start us, length us, event | category | flops | bytes accessed | tf_op | source)
XLA Modules:
  0.0 22.4 jit_solution(5710893167788164635)
XLA Ops:
  0.0 20.3 %shard_map.28 = f32[3,2,256,128]{3,2,1,0:T(8,128)} custom-call(f32[2,256,128]{2,1,0:T(8,128)} %visc_hbm.1, f32[3,2,256,128]{3,2,1,0:T(8,128)} %vel_hbm.1), custom_call_target="tpu_custom_call" | custom-call | tf_op jit(solution)/shard_map/pallas_call | solution.py:354
  20.3 2.1 %copy.4 = f32[3,2,256,128]{3,2,1,0:T(8,128)} copy(f32[3,2,256,128]{3,2,1,0:T(8,128)} %shard_map.28) | data formatting | bytes 1572864

commit v2 on v1

--- a/solution.py
+++ b/solution.py
@@ -155,11 +155,11 @@
 
 def kernel(
     nx, ny, sx, sy,
-    visc_hbm, vel_hbm, out_hbm,
-    visc, vel, eps, eps_t, out,
+    visc_hbm, vel_hbm, ypart, yphi, ypsi, yends_out,
+    visc, vel, eps, eps_t,
     xphi, xpsi, xaw, xbw, xends, xstates, xtots, xpart, xnodes, xwts, xcoef, xsrc,
-    yphi, ypsi, yaw, ybw, yends, ystates, ytots, ypart, ynodes, ywts, ycoef, ysrc,
-    ut, in_sem, out_sem,
+    yaw, ybw, yends, ystates, ytots, ynodes, ywts, ycoef, ysrc,
+    ut, in_sem,
     xc_send, xc_recv, xs_send, xs_recv, yc_send, yc_recv, ys_send, ys_recv,
 ):
     gx = lax.axis_index("gx")
@@ -298,32 +298,32 @@
     interior(vel_y, yphi, ypsi, yaw, ybw, ytots, ypart, 4, sy)
 
     arrive("gy", gy, ny, ysrc, ys_send, ys_recv)
-    ends = []
     for side in range(2):
-        tiles = []
         for c in range(3):
             acc = ywts[side, 0] * ysrc[0, c]
             for p in range(1, ny):
                 acc = acc + ywts[side, p] * ysrc[p, c]
-            tiles.append(acc + pltpu.roll(acc, 4, 0))
-        ends.append(tiles)
+            yends_out[side, c] = acc + pltpu.roll(acc, 4, 0)
+    for copy in sent:
+        copy.wait_send()
+
+
+def finish(sy, ypart, yphi, ypsi, ends, out_hbm, turned, out, sem):
     stores = []
     for c in range(3):
         for z in range(2):
             for tile in range(2):
                 col = 2 * z + tile
-                s = row8(ends[0][c][col : col + 1, :])
-                r = row8(ends[1][c][col : col + 1, :])
+                s = row8(ends[0, c, col : col + 1, :])
+                r = row8(ends[1, c, col : col + 1, :])
                 for t in range(sy):
-                    ut[c, col, pl.ds(t, CH, stride=sy), :] = (
+                    turned[c, col, pl.ds(t, CH, stride=sy), :] = (
                         ypart[c, col, t] + yphi[col, t] * s + ypsi[col, t] * r
                     )
-                out[c, z, tile * LANES : (tile + 1) * LANES, :] = ut[c, col].T
-            store = pltpu.make_async_copy(out.at[c, z], out_hbm.at[c, z], out_sem.at[2 * c + z])
+                out[c, z, tile * LANES : (tile + 1) * LANES, :] = turned[c, col].T
+            store = pltpu.make_async_copy(out.at[c, z], out_hbm.at[c, z], sem.at[2 * c + z])
             store.start()
             stores.append(store)
-    for copy in sent:
-        copy.wait_send()
     for store in stores:
         store.wait()
 
@@ -339,39 +339,64 @@
         return [
             vm(cols, steps, CH, LANES),
             vm(cols, steps, CH, LANES),
-            vm(cols, steps, CH, LANES),
-            vm(cols, steps, CH, LANES),
             vm(4, cols, CH, LANES),
             vm(4, cols, CH, LANES),
             vm(2, 3, cols, CH, LANES),
-            vm(3, cols, steps, CH, LANES),
             vm(2, devices + 1, rows, LANES),
             vm(2, devices, CH, LANES),
             vm(devices, coefs, LANES),
             vm(devices, srcs, CH, LANES),
         ]
 
-    return pl.pallas_call(
+    on_chip = pl.BlockSpec(memory_space=pltpu.VMEM)
+    in_hbm = pl.BlockSpec(memory_space=pltpu.HBM)
+    shape = lambda *dims: jax.ShapeDtypeStruct(dims, f32)
+    xphase = phase(2, sx, nx, 2, 8, 2)
+    kept = pl.pallas_call(
         functools.partial(kernel, nx, ny, sx, sy),
-        out_shape=jax.ShapeDtypeStruct(velocity.shape, f32),
-        in_specs=[pl.BlockSpec(memory_space=pl.ANY)] * 2,
-        out_specs=pl.BlockSpec(memory_space=pl.ANY),
+        out_shape=(
+            shape(3, 4, sy, CH, LANES),
+            shape(4, sy, CH, LANES),
+            shape(4, sy, CH, LANES),
+            shape(2, 3, CH, LANES),
+        ),
+        in_specs=[in_hbm] * 2,
+        out_specs=(on_chip,) * 4,
         scratch_shapes=[
             vm(2, lx, ly),
             vm(3, 2, lx, ly),
             vm(2, lx, ly),
             vm(4, ly, LANES),
-            vm(3, 2, lx, ly),
-            *phase(2, sx, nx, 2, 8, 2),
+            vm(2, sx, CH, LANES),
+            vm(2, sx, CH, LANES),
+            *xphase[:5],
+            vm(3, 2, sx, CH, LANES),
+            *xphase[5:],
             *phase(4, sy, ny, 4, 16, 3),
             vm(3, 4, ly, LANES),
             dma(8),
-            dma(6),
             dma(nx), dma(nx), dma(nx), dma(nx),
             dma(ny), dma(ny), dma(ny), dma(ny),
         ],
-        compiler_params=pltpu.CompilerParams(collective_id=0, has_side_effects=True),
-    )(viscosity, velocity)
+        compiler_params=pltpu.CompilerParams(
+            collective_id=0, has_side_effects=True, vmem_limit_bytes=24 * 2**20
+        ),
+    )(
+        pltpu.with_memory_space_constraint(viscosity, pltpu.HBM),
+        pltpu.with_memory_space_constraint(velocity, pltpu.HBM),
+    )
+    return pl.pallas_call(
+        functools.partial(finish, sy),
+        out_shape=shape(*velocity.shape),
+        in_specs=[on_chip] * 4,
+        out_specs=in_hbm,
+        scratch_shapes=[
+            vm(3, 4, ly, LANES),
+            vm(3, 2, lx, ly),
+            dma(6),
+        ],
+        compiler_params=pltpu.CompilerParams(vmem_limit_bytes=16 * 2**20),
+    )(*kept)
 
 
 def solution(mesh):

time: 22.6 us -> 20.5 us (0.907)
  local copies, waits for them, and re-layouts: 2.06 us -> 0 us
    unnamed x1 -> x0, local copies, waits for them, and re-layouts: 2.06 us -> none
    pallas_call x1 -> x2, Pallas kernels: 20.3 us -> 20.4 us  [the longest x1 19.2 us: on_device(): pl.pallas_call(functools.partial(kernel, nx, ny, sx, sy), out_shape=(shap...]
where the time goes in v2:
time: 20.5 us; the launch traced here: 20.4 us
  Pallas kernels  20.4 us (100%)
    pallas_call x1, Pallas kernels, on_device(): pl.pallas_call(functools.partial(kernel, nx, ny, sx, sy), out_shape=(shap...  19.2 us
    pallas_call x1, Pallas kernels, on_device(): pl.pallas_call(functools.partial(finish, sy), out_shape=shape(*velocity.s...  1.17 us

profile of v2, /device:TPU:1, one launch (start us, length us, event | category | flops | bytes accessed | tf_op | source)
XLA Modules:
  0.0 20.4 jit_solution(9317075512670754296)
XLA Ops:
  0.0 19.2 %shard_map.28 = (f32[3,4,16,8,128]{4,3,2,1,0:T(8,128)S(1)}, f32[4,16,8,128]{3,2,1,0:T(8,128)S(1)}, f32[4,16,8,128]{3,2,1,0:T(8,128)S(1)}, f32[2,3,8,128]{3,2,1,0:T(8,128)S(1)}) custom-call(f32[2,256,128]{2,1,0:T(8,128)} %visc_hbm.1, f32[3,2,256,128]{3,2,1,0:T(8,128)} %vel_hbm.1), custom_call_target="tpu_custom_call" | custom-call | tf_op jit(solution)/shard_map/pallas_call | solution.py:355
  19.2 1.2 %shard_map.29 = f32[3,2,256,128]{3,2,1,0:T(8,128)} custom-call(f32[3,4,16,8,128]{4,3,2,1,0:T(8,128)S(1)} %get-tuple-element.9.ypart, f32[4,16,8,128]{3,2,1,0:T(8,128)S(1)} %get-tuple-element.10.yphi, f32[4,16,8,128]{3,2,1,0:T(8,128)S(1)} %get-tuple-element.11.ypsi, f32[2,3,8,128]{3,2,1,0:T(8,128)S(1)} %get-tuple-element.12.ends), custom_call_target="tpu_custom_call" | custom-call | tf_op jit(solution)/shard_map/pallas_call | solution.py:388

commit v3 on v2

--- a/solution.py
+++ b/solution.py
@@ -11,6 +11,21 @@
 MESH = pl.DeviceIdType.MESH
 CH = 8
 LANES = 128
+
+
+NEAR = 4
+
+
+def ring_peers(me, devices, inner):
+    outer = devices // inner
+    mine_out, mine_in = me // inner, lax.rem(me, inner)
+    far = lambda step, size: min(step, size - step) if size > 2 else 0
+    steps = [(a, b) for a in range(outer) for b in range(inner) if a or b]
+    steps.sort(key=lambda ab: -(far(ab[0], outer) + far(ab[1], inner)))
+    return [
+        (a, b, lax.rem(mine_out + a, outer) * inner + lax.rem(mine_in + b, inner))
+        for a, b in steps
+    ]
 
 
 def row8(ref_or_value):
@@ -159,7 +174,7 @@
     visc, vel, eps, eps_t,
     xphi, xpsi, xaw, xbw, xends, xstates, xtots, xpart, xnodes, xwts, xcoef, xsrc,
     yaw, ybw, yends, ystates, ytots, ynodes, ywts, ycoef, ysrc,
-    ut, in_sem,
+    ut, in_sem, entered,
     xc_send, xc_recv, xs_send, xs_recv, yc_send, yc_recv, ys_send, ys_recv,
 ):
     gx = lax.axis_index("gx")
@@ -175,23 +190,22 @@
     for copy in loads:
         copy.start()
     barrier = pltpu.get_barrier_semaphore()
-    for d in range(1, nx):
-        pl.semaphore_signal(
-            barrier, inc=1, device_id={"gx": lax.rem(gx + d, nx)}, device_id_type=MESH
-        )
-    for d in range(1, ny):
-        pl.semaphore_signal(
-            barrier, inc=1, device_id={"gy": lax.rem(gy + d, ny)}, device_id_type=MESH
-        )
-
-    def share(axis, me, devices, buf, send, recv):
+    xpeers = ring_peers(gx, nx, 2)
+    ypeers = ring_peers(gy, ny, NEAR)
+    inner = [peer for a, b, peer in ypeers if a == 0]
+    outer = [peer for a, b, peer in ypeers if b == 0]
+    for a, b, peer in xpeers:
+        pl.semaphore_signal(barrier, inc=1, device_id={"gx": peer}, device_id_type=MESH)
+    for peer in inner + outer:
+        pl.semaphore_signal(barrier, inc=1, device_id={"gy": peer}, device_id_type=MESH)
+
+    def share(axis, me, peers, buf, send, recv):
         copies = []
-        for d in range(1, devices):
-            peer = lax.rem(me + d, devices)
+        for d, (a, b, peer) in enumerate(peers):
             copy = pltpu.make_async_remote_copy(
                 src_ref=buf.at[me],
                 dst_ref=buf.at[me],
-                send_sem=send.at[d - 1],
+                send_sem=send.at[d],
                 recv_sem=recv.at[me],
                 device_id={axis: peer},
                 device_id_type=MESH,
@@ -200,13 +214,12 @@
             copies.append(copy)
         return copies
 
-    def arrive(axis, me, devices, buf, send, recv):
-        for d in range(1, devices):
-            peer = lax.rem(me + d, devices)
+    def arrive(axis, peers, buf, send, recv):
+        for d, (a, b, peer) in enumerate(peers):
             pltpu.make_async_remote_copy(
                 src_ref=buf.at[peer],
                 dst_ref=buf.at[peer],
-                send_sem=send.at[d - 1],
+                send_sem=send.at[d],
                 recv_sem=recv.at[peer],
                 device_id={axis: peer},
                 device_id_type=MESH,
@@ -231,8 +244,10 @@
 
     fundamental(eps_x, xphi, xpsi, xends, 2, sx)
     xwhole, xinv = chunk_states(xends, xstates, xcoef.at[gx], 2)
-    pl.semaphore_wait(barrier, nx + ny - 2)
-    sent = share("gx", gx, nx, xcoef, xc_send, xc_recv)
+    pl.semaphore_wait(barrier, nx - 1 + len(inner) + len(outer))
+    for peer in outer:
+        pl.semaphore_signal(entered, inc=1, device_id={"gy": peer}, device_id_type=MESH)
+    sent = share("gx", gx, xpeers, xcoef, xc_send, xc_recv)
     weights(eps_x, xphi, xpsi, xaw, xbw, xstates, xwhole, xinv, 2, sx)
     for copy in loads[2:]:
         copy.wait()
@@ -247,20 +262,21 @@
                 row = k * jnp.sum(value, axis=0, keepdims=True)
                 xsrc[gx, c // 2, at : at + 1, :] = row
     xsrc[gx, 1, 4:8, :] = jnp.zeros((4, LANES), jnp.float32)
-    sent += share("gx", gx, nx, xsrc, xs_send, xs_recv)
+    sent += share("gx", gx, xpeers, xsrc, xs_send, xs_recv)
 
     for z in range(2):
         for tile in range(2):
             eps_t[2 * z + tile] = eps[z, tile * LANES : (tile + 1) * LANES, :].T
     fundamental(eps_y, yphi, ypsi, yends, 4, sy)
     ywhole, yinv = chunk_states(yends, ystates, ycoef.at[gy], 4)
-    sent += share("gy", gy, ny, ycoef, yc_send, yc_recv)
     interior(vel_x, xphi, xpsi, xaw, xbw, xtots, xpart, 2, sx)
+    pl.semaphore_wait(entered, len(outer))
+    sent += share("gy", gy, ypeers, ycoef, yc_send, yc_recv)
     weights(eps_y, yphi, ypsi, yaw, ybw, ystates, ywhole, yinv, 4, sy)
-    arrive("gx", gx, nx, xcoef, xc_send, xc_recv)
+    arrive("gx", xpeers, xcoef, xc_send, xc_recv)
     green(xcoef, xnodes, xwts, gx, nx, 2)
 
-    arrive("gx", gx, nx, xsrc, xs_send, xs_recv)
+    arrive("gx", xpeers, xsrc, xs_send, xs_recv)
     ends = []
     for side in range(2):
         tiles = []
@@ -292,12 +308,12 @@
             for lr, value in enumerate((left[c], right[c])):
                 at = lr * 4 + col
                 ysrc[gy, c, at : at + 1, :] = k * jnp.sum(value, axis=0, keepdims=True)
-    sent += share("gy", gy, ny, ysrc, ys_send, ys_recv)
-    arrive("gy", gy, ny, ycoef, yc_send, yc_recv)
+    sent += share("gy", gy, ypeers, ysrc, ys_send, ys_recv)
+    arrive("gy", ypeers, ycoef, yc_send, yc_recv)
     green(ycoef, ynodes, ywts, gy, ny, 4)
     interior(vel_y, yphi, ypsi, yaw, ybw, ytots, ypart, 4, sy)
 
-    arrive("gy", gy, ny, ysrc, ys_send, ys_recv)
+    arrive("gy", ypeers, ysrc, ys_send, ys_recv)
     for side in range(2):
         for c in range(3):
             acc = ywts[side, 0] * ysrc[0, c]
@@ -375,6 +391,7 @@
             *phase(4, sy, ny, 4, 16, 3),
             vm(3, 4, ly, LANES),
             dma(8),
+            pltpu.SemaphoreType.REGULAR,
             dma(nx), dma(nx), dma(nx), dma(nx),
             dma(ny), dma(ny), dma(ny), dma(ny),
         ],

time: 20.5 us -> 19.5 us (0.951)
  Pallas kernels: 20.4 us -> 19.4 us
    pallas_call x1, Pallas kernels: 19.2 us -> 18.2 us  [on_device(): pl.pallas_call(functools.partial(kernel, nx, ny, sx, sy), out_shape=(shap...]
where the time goes in v3:
time: 19.5 us; the launch traced here: 19.4 us
  Pallas kernels  19.4 us (99%)
    pallas_call x1, Pallas kernels, on_device(): pl.pallas_call(functools.partial(kernel, nx, ny, sx, sy), out_shape=(shap...  18.2 us
    pallas_call x1, Pallas kernels, on_device(): pl.pallas_call(functools.partial(finish, sy), out_shape=shape(*velocity.s...  1.17 us

profile of v3, /device:TPU:1, one launch (start us, length us, event | category | flops | bytes accessed | tf_op | source)
XLA Modules:
  0.0 19.4 jit_solution(4263312234930333702)
XLA Ops:
  0.0 18.2 %shard_map.28 = (f32[3,4,16,8,128]{4,3,2,1,0:T(8,128)S(1)}, f32[4,16,8,128]{3,2,1,0:T(8,128)S(1)}, f32[4,16,8,128]{3,2,1,0:T(8,128)S(1)}, f32[2,3,8,128]{3,2,1,0:T(8,128)S(1)}) custom-call(f32[2,256,128]{2,1,0:T(8,128)} %visc_hbm.1, f32[3,2,256,128]{3,2,1,0:T(8,128)} %vel_hbm.1), custom_call_target="tpu_custom_call" | custom-call | tf_op jit(solution)/shard_map/pallas_call | solution.py:371
  18.2 1.2 %shard_map.29 = f32[3,2,256,128]{3,2,1,0:T(8,128)} custom-call(f32[3,4,16,8,128]{4,3,2,1,0:T(8,128)S(1)} %get-tuple-element.9.ypart, f32[4,16,8,128]{3,2,1,0:T(8,128)S(1)} %get-tuple-element.10.yphi, f32[4,16,8,128]{3,2,1,0:T(8,128)S(1)} %get-tuple-element.11.ypsi, f32[2,3,8,128]{3,2,1,0:T(8,128)S(1)} %get-tuple-element.12.ends), custom_call_target="tpu_custom_call" | custom-call | tf_op jit(solution)/shard_map/pallas_call | solution.py:405

commit v4 on v3

v4 whole, which is shorter than its diff:
```python
import functools

import jax
import jax.numpy as jnp
from jax import lax
from jax.experimental import pallas as pl
from jax.experimental.pallas import tpu as pltpu
from jax.sharding import PartitionSpec as P

diffusion = 10000.0
MESH = pl.DeviceIdType.MESH
CH = 8
LANES = 128


NEAR = 4


def ring_peers(me, devices, inner):
    outer = devices // inner
    mine_out, mine_in = me // inner, lax.rem(me, inner)
    far = lambda step, size: min(step, size - step) if size > 2 else 0
    steps = [(a, b) for a in range(outer) for b in range(inner) if a or b]
    steps.sort(key=lambda ab: -(far(ab[0], outer) + far(ab[1], inner)))
    return [
        (a, b, lax.rem(mine_out + a, outer) * inner + lax.rem(mine_in + b, inner))
        for a, b in steps
    ]


def row8(ref_or_value):
    return jnp.broadcast_to(ref_or_value, (CH, LANES))


def fundamental(eps, phi, psi, ends, cols, steps):
    one = jnp.ones((CH, LANES), jnp.float32)
    zero = jnp.zeros((CH, LANES), jnp.float32)
    state = [(one, zero, zero, one) for _ in range(cols)]
    for t in range(steps):
        for col in range(cols):
            a, da, b, db = state[col]
            phi[col, t] = a
            psi[col, t] = b
            e = eps[col, pl.ds(t, CH, stride=steps + 1), :]
            da = da + e * a
            db = db + e * b
            state[col] = (a + da, da, b + db, db)
    for col in range(cols):
        a, da, b, db = state[col]
        ends[0, col] = a
        ends[1, col] = b
        ends[2, col] = da
        ends[3, col] = db


def chunk_states(ends, states, coef, cols):
    one = jnp.ones((cols, LANES), jnp.float32)
    zero = jnp.zeros((cols, LANES), jnp.float32)
    f, df, m, v = one, zero, zero, one
    n, z = zero, one
    for q in range(CH):
        a, b, da, db = [ends[k, :, q, :] for k in range(4)]
        states[0, :, q, :] = m
        states[1, :, q, :] = v
        f, df = a * f + b * df, da * f + db * df
        m, v = a * m + b * v, da * m + db * v
        r = CH - 1 - q
        a, b, da, db = [ends[k, :, r, :] for k in range(4)]
        n, z = db * n + b * z, a * z + da * n
        states[2, :, r, :] = n
        states[3, :, r, :] = z
    coef[0 * cols : 1 * cols, :] = f
    coef[1 * cols : 2 * cols, :] = m
    coef[2 * cols : 3 * cols, :] = df
    coef[3 * cols : 4 * cols, :] = v
    return m, 1.0 / m


def weights(phi, psi, alpha, beta, states, inverse, cols, steps):
    pitch = steps + 1
    for col in range(cols):
        k = row8(inverse[col : col + 1, :])
        ms, vs, ns, zs = [states[j, col] * k for j in range(4)]
        for t in range(steps):
            a = phi[col, t]
            b = psi[col, t]
            alpha[col, pl.ds(t, CH, stride=pitch), :] = ns * a - zs * b
            beta[col, pl.ds(t, CH, stride=pitch), :] = ms * a + vs * b


def tile_rows(m, steps):
    per = steps // CH
    return pl.ds((m // per) * (steps + 1) + (m % per) * CH, CH)


def totals(load_f, eps, alpha, beta, steps, col, comps=range(3)):
    zero = jnp.zeros((CH, LANES), jnp.float32)
    left = [zero] * 3
    right = [zero] * 3
    for m in range(steps):
        rows = tile_rows(m, steps)
        e = eps[col, rows, :]
        a = alpha[col, rows, :]
        b = beta[col, rows, :]
        for c in comps:
            h = load_f(c, m) * e
            left[c] = left[c] + a * h
            right[c] = right[c] + b * h
    return left, right


def scan_up(x, places):
    for d in (1, 2, 4):
        x = x + jnp.where(places >= d, pltpu.roll(x, d, 0), 0.0)
    return x


def scan_down(x, places):
    for d in (1, 2, 4):
        x = x + jnp.where(places < CH - d, pltpu.roll(x, CH - d, 0), 0.0)
    return x


def interior(f, eps, alpha, beta, whole, part, cols, steps):
    pitch = steps + 1
    places = lax.broadcasted_iota(jnp.int32, (CH, LANES), 0)
    zero = jnp.zeros((CH, LANES), jnp.float32)
    for col in range(cols):
        w = row8(whole[col : col + 1, :])
        left = [zero] * 3
        right = [zero] * 3
        for t in range(steps):
            rows = pl.ds(t, CH, stride=pitch)
            we = eps[col, rows, :] * w
            aw, bw = alpha[col, rows, :] * we, beta[col, rows, :] * we
            for c in range(3):
                left[c] = left[c] + aw * f[c, col, rows, :]
                right[c] = right[c] + bw * f[c, col, rows, :]
        pre = [scan_up(right[c], places) - right[c] for c in range(3)]
        suf = [scan_down(left[c], places) for c in range(3)]
        for t in range(steps):
            rows = pl.ds(t, CH, stride=pitch)
            we = eps[col, rows, :] * w
            al, be = alpha[col, rows, :], beta[col, rows, :]
            for c in range(3):
                h = f[c, col, rows, :] * we
                pre[c] = pre[c] + be * h
                suf[c] = suf[c] - al * h
                part[c, col, rows, :] = al * pre[c] + be * suf[c]


def green(coef, nodes, wts, me, devices, rows):
    m = jnp.ones((rows, LANES), jnp.float32)
    v = m
    n = jnp.zeros((rows, LANES), jnp.float32)
    z = jnp.ones((rows, LANES), jnp.float32)
    ms, ns = [m], [n]
    nodes[0, 0] = m
    nodes[1, devices] = n
    for p in range(devices):
        a, b, da, db = [coef[p, k * rows : (k + 1) * rows, :] for k in range(4)]
        m, v = a * m + b * v, da * m + db * v
        ms.append(m)
        nodes[0, p + 1] = m
        r = devices - 1 - p
        a, b, da, db = [coef[r, k * rows : (k + 1) * rows, :] for k in range(4)]
        n, z = db * n + b * z, a * z + da * n
        ns.append(n)
        nodes[1, r] = n
    ns = ns[::-1]
    inverse = 1.0 / m
    for side in range(2):
        at = me + side
        mm = nodes[0, at] * inverse
        nn = nodes[1, at] * inverse
        g = [jnp.where(p <= at, ms[p] * nn, ns[p] * mm) for p in range(devices + 1)]
        for p in range(devices):
            pair = [g[p], g[p + 1]] * (CH // (2 * rows))
            wts[side, p] = jnp.concatenate(pair, axis=0)


def kernel(
    nx, ny, sx, sy,
    visc_hbm, vel_hbm, ypart, yalpha, ybeta, yends_out,
    visc, vel, eps, eps_t, velp, ut,
    xphi, xpsi, xalpha, xbeta, xends, xstates, xpart, xnodes, xwts, xcoef, xsrc,
    yphi, ypsi, yends, ystates, ynodes, ywts, ycoef, ysrc,
    in_sem, entered, sems,
):
    gx = lax.axis_index("gx")
    gy = lax.axis_index("gy")
    for z in range(2):
        pltpu.make_async_copy(visc_hbm.at[z], visc.at[z], in_sem.at[0]).start()
    for c in range(3):
        for z in range(2):
            pltpu.make_async_copy(vel_hbm.at[c, z], vel.at[c, z], in_sem.at[1]).start()
    barrier = pltpu.get_barrier_semaphore()
    xpeers = ring_peers(gx, nx, 2)
    ypeers = ring_peers(gy, ny, NEAR)
    inner = [peer for a, b, peer in ypeers if a == 0]
    outer = [peer for a, b, peer in ypeers if b == 0]
    for a, b, peer in xpeers:
        pl.semaphore_signal(barrier, inc=1, device_id={"gx": peer}, device_id_type=MESH)
    for peer in inner + outer:
        pl.semaphore_signal(barrier, inc=1, device_id={"gy": peer}, device_id_type=MESH)

    def share(axis, me, peers, buf, sem):
        for a, b, peer in peers:
            pltpu.make_async_remote_copy(
                src_ref=buf.at[me],
                dst_ref=buf.at[me],
                send_sem=sems.at[sem, 0],
                recv_sem=sems.at[sem, 1],
                device_id={axis: peer},
                device_id_type=MESH,
            ).start()

    def all_of(axis, peers, buf, sem):
        return pltpu.make_async_remote_copy(
            src_ref=buf.at[pl.ds(0, len(peers))],
            dst_ref=buf.at[pl.ds(0, len(peers))],
            send_sem=sems.at[sem, 0],
            recv_sem=sems.at[sem, 1],
            device_id={axis: peers[0][2]},
            device_id_type=MESH,
        )

    tx, ty = sx, sy
    pltpu.make_async_copy(visc_hbm, visc, in_sem.at[0]).wait()
    for z in range(2):
        for m in range(tx):
            eps[z, tile_rows(m, sx), :] = 1.0 / (diffusion * visc[z, m * CH : (m + 1) * CH, :])

    fundamental(eps, xphi, xpsi, xends, 2, sx)
    xwhole, xinv = chunk_states(xends, xstates, xcoef.at[gx], 2)
    pl.semaphore_wait(barrier, nx - 1 + len(inner) + len(outer))
    share("gx", gx, xpeers, xcoef, 0)
    weights(xphi, xpsi, xalpha, xbeta, xstates, xinv, 2, sx)
    pltpu.make_async_copy(vel_hbm, vel, in_sem.at[1]).wait()
    for col in range(2):
        left, right = totals(
            lambda c, m: vel[c, col, m * CH : (m + 1) * CH, :], eps, xalpha, xbeta, sx, col
        )
        for c in range(3):
            for lr, value in enumerate((left[c], right[c])):
                at = (c % 2) * 4 + lr * 2 + col
                xsrc[gx, c // 2, at : at + 1, :] = jnp.sum(value, axis=0, keepdims=True)
    xsrc[gx, 1, 4:8, :] = jnp.zeros((4, LANES), jnp.float32)
    share("gx", gx, xpeers, xsrc, 1)
    for peer in outer:
        pl.semaphore_signal(entered, inc=1, device_id={"gy": peer}, device_id_type=MESH)

    half = LANES // CH
    for z in range(2):
        for tile in range(2):
            turned = jnp.concatenate(
                [eps[z, tile_rows(tile * half + m, sx), :] for m in range(half)], axis=0
            ).T
            for m in range(ty):
                eps_t[2 * z + tile, tile_rows(m, sy), :] = turned[m * CH : (m + 1) * CH, :]
    fundamental(eps_t, yphi, ypsi, yends, 4, sy)
    ywhole, yinv = chunk_states(yends, ystates, ycoef.at[gy], 4)
    for c in range(3):
        for z in range(2):
            for m in range(tx):
                velp[c, z, tile_rows(m, sx), :] = vel[c, z, m * CH : (m + 1) * CH, :]
    pl.semaphore_wait(entered, len(outer))
    share("gy", gy, ypeers, ycoef, 2)
    interior(velp, eps, xalpha, xbeta, xwhole, xpart, 2, sx)
    weights(yphi, ypsi, yalpha, ybeta, ystates, yinv, 4, sy)
    all_of("gx", xpeers, xcoef, 0).wait_recv()
    green(xcoef, xnodes, xwts, gx, nx, 2)

    all_of("gx", xpeers, xsrc, 1).wait_recv()
    ends = []
    for side in range(2):
        tiles = []
        for k in range(2):
            acc = xwts[side, 0] * xsrc[0, k]
            for p in range(1, nx):
                acc = acc + xwts[side, p] * xsrc[p, k]
            tiles.append(acc + pltpu.roll(acc, CH - 2, 0))
        ends.append(tiles)
    for z in range(2):
        for tile in range(2):
            col = 2 * z + tile
            turned = []
            for c in range(3):
                at = (c % 2) * 4 + z
                s = row8(ends[0][c // 2][at : at + 1, :])
                r = row8(ends[1][c // 2][at : at + 1, :])
                block = []
                for m in range(half):
                    rows = tile_rows(tile * half + m, sx)
                    block.append(
                        xpart[c, z, rows, :] + xalpha[z, rows, :] * s + xbeta[z, rows, :] * r
                    )
                turned.append(jnp.concatenate(block, axis=0).T)
                for m in range(ty):
                    ut[c, col, tile_rows(m, sy), :] = turned[c][m * CH : (m + 1) * CH, :]
            left, right = totals(
                lambda c, m: turned[c][m * CH : (m + 1) * CH, :],
                eps_t, yalpha, ybeta, sy, col,
            )
            for c in range(3):
                for lr, value in enumerate((left[c], right[c])):
                    at = lr * 4 + col
                    ysrc[gy, c, at : at + 1, :] = jnp.sum(value, axis=0, keepdims=True)
    share("gy", gy, ypeers, ysrc, 3)
    all_of("gy", ypeers, ycoef, 2).wait_recv()
    green(ycoef, ynodes, ywts, gy, ny, 4)
    interior(ut, eps_t, yalpha, ybeta, ywhole, ypart, 4, sy)
    all_of("gx", xpeers, xcoef, 0).wait_send()
    all_of("gx", xpeers, xsrc, 1).wait_send()
    all_of("gy", ypeers, ycoef, 2).wait_send()

    all_of("gy", ypeers, ysrc, 3).wait_recv()
    for side in range(2):
        for c in range(3):
            acc = ywts[side, 0] * ysrc[0, c]
            for p in range(1, ny):
                acc = acc + ywts[side, p] * ysrc[p, c]
            yends_out[side, c] = acc + pltpu.roll(acc, 4, 0)
    all_of("gy", ypeers, ysrc, 3).wait_send()


def finish(sy, ypart, yalpha, ybeta, ends, out_hbm, out, sem):
    stores = []
    for c in range(3):
        for z in range(2):
            for tile in range(2):
                col = 2 * z + tile
                s = row8(ends[0, c, col : col + 1, :])
                r = row8(ends[1, c, col : col + 1, :])
                block = []
                for m in range(sy):
                    rows = tile_rows(m, sy)
                    block.append(
                        ypart[c, col, rows, :] + yalpha[col, rows, :] * s + ybeta[col, rows, :] * r
                    )
                out[c, z, tile * LANES : (tile + 1) * LANES, :] = jnp.concatenate(block, axis=0).T
            store = pltpu.make_async_copy(out.at[c, z], out_hbm.at[c, z], sem.at[2 * c + z])
            store.start()
            stores.append(store)
    for store in stores:
        store.wait()


def on_device(nx, ny, velocity, viscosity):
    lx, ly = velocity.shape[2], velocity.shape[3]
    sx, sy = lx // CH, ly // CH
    f32 = jnp.float32
    vm = lambda *shape: pltpu.VMEM(shape, f32)
    dma = lambda n: pltpu.SemaphoreType.DMA((n,))

    padx, pady = CH * (sx + 1), CH * (sy + 1)

    on_chip = pl.BlockSpec(memory_space=pltpu.VMEM)
    in_hbm = pl.BlockSpec(memory_space=pltpu.HBM)
    shape = lambda *dims: jax.ShapeDtypeStruct(dims, f32)
    kept = pl.pallas_call(
        functools.partial(kernel, nx, ny, sx, sy),
        out_shape=(
            shape(3, 4, pady, LANES),
            shape(4, pady, LANES),
            shape(4, pady, LANES),
            shape(2, 3, CH, LANES),
        ),
        in_specs=[in_hbm] * 2,
        out_specs=(on_chip,) * 4,
        scratch_shapes=[
            vm(2, lx, ly),
            vm(3, 2, lx, ly),
            vm(2, padx, LANES),
            vm(4, pady, LANES),
            vm(3, 2, padx, LANES),
            vm(3, 4, pady, LANES),
            vm(2, sx, CH, LANES),
            vm(2, sx, CH, LANES),
            vm(2, padx, LANES),
            vm(2, padx, LANES),
            vm(4, 2, CH, LANES),
            vm(4, 2, CH, LANES),
            vm(3, 2, padx, LANES),
            vm(2, nx + 1, 2, LANES),
            vm(2, nx, CH, LANES),
            vm(nx, 8, LANES),
            vm(nx, 2, CH, LANES),
            vm(4, sy, CH, LANES),
            vm(4, sy, CH, LANES),
            vm(4, 4, CH, LANES),
            vm(4, 4, CH, LANES),
            vm(2, ny + 1, 4, LANES),
            vm(2, ny, CH, LANES),
            vm(ny, 16, LANES),
            vm(ny, 3, CH, LANES),
            dma(2),
            pltpu.SemaphoreType.REGULAR,
            pltpu.SemaphoreType.DMA((4, 2)),
        ],
        compiler_params=pltpu.CompilerParams(
            collective_id=0, has_side_effects=True, vmem_limit_bytes=24 * 2**20
        ),
    )(
        pltpu.with_memory_space_constraint(viscosity, pltpu.HBM),
        pltpu.with_memory_space_constraint(velocity, pltpu.HBM),
    )
    return pl.pallas_call(
        functools.partial(finish, sy),
        out_shape=shape(*velocity.shape),
        in_specs=[on_chip] * 4,
        out_specs=in_hbm,
        scratch_shapes=[
            vm(3, 2, lx, ly),
            dma(6),
        ],
        compiler_params=pltpu.CompilerParams(vmem_limit_bytes=16 * 2**20),
    )(*kept)


def solution(mesh):
    return jax.shard_map(
        functools.partial(on_device, mesh.shape["gx"], mesh.shape["gy"]),
        mesh=mesh,
        in_specs=(P(None, None, "gx", "gy"), P(None, "gx", "gy")),
        out_specs=P(None, None, "gx", "gy"),
        check_vma=False,
    )
```

time: 19.5 us -> 17.2 us (0.88)
  Pallas kernels: 19.4 us -> 17.1 us
    pallas_call x1, Pallas kernels: 18.2 us -> 16.1 us  [on_device(): pl.pallas_call(functools.partial(kernel, nx, ny, sx, sy), out_shape=(shap...]
where the time goes in v4:
time: 17.2 us; the launch traced here: 17.1 us
  Pallas kernels  17.1 us (99%)
    pallas_call x1, Pallas kernels, on_device(): pl.pallas_call(functools.partial(kernel, nx, ny, sx, sy), out_shape=(shap...  16.1 us
    pallas_call x1, Pallas kernels, on_device(): pl.pallas_call(functools.partial(finish, sy), out_shape=shape(*velocity.s...  1.03 us

profile of v4, /device:TPU:1, one launch (start us, length us, event | category | flops | bytes accessed | tf_op | source)
XLA Modules:
  0.0 17.1 jit_solution(13163743485331582301)
XLA Ops:
  0.0 16.1 %shard_map.28 = (f32[3,4,136,128]{3,2,1,0:T(8,128)S(1)}, f32[4,136,128]{2,1,0:T(8,128)S(1)}, f32[4,136,128]{2,1,0:T(8,128)S(1)}, f32[2,3,8,128]{3,2,1,0:T(8,128)S(1)}) custom-call(f32[2,256,128]{2,1,0:T(8,128)} %visc_hbm.1, f32[3,2,256,128]{3,2,1,0:T(8,128)} %vel_hbm.1), custom_call_target="tpu_custom_call" | custom-call | tf_op jit(solution)/shard_map/pallas_call | solution.py:361
  16.1 1.0 %shard_map.29 = f32[3,2,256,128]{3,2,1,0:T(8,128)} custom-call(f32[3,4,136,128]{3,2,1,0:T(8,128)S(1)} %get-tuple-element.9.ypart, f32[4,136,128]{2,1,0:T(8,128)S(1)} %get-tuple-element.10.yalpha, f32[4,136,128]{2,1,0:T(8,128)S(1)} %get-tuple-element.11.ybeta, f32[2,3,8,128]{3,2,1,0:T(8,128)S(1)} %get-tuple-element.12.ends), custom_call_target="tpu_custom_call" | custom-call | tf_op jit(solution)/shard_map/pallas_call | solution.py:408
